TPU v7x, 32 devices: a whole 2x2x4 slice. The times are simulated.
32 devices in a mesh: ctx: 8 (over y, x, core), chan: 4 (over z).
Axes of the slice: x: 2, y: 2, z: 4, core: 2. Of those that a mesh axis runs over, the one named last changes fastest.
Arguments:
- features: bfloat16 [3, 8192, 4096], P(None, 'chan', 'ctx'), may hold values from -6 to 6
- short_filter: float32 [3, 3, 8192], P(None, None, 'chan'), may hold values from -3.5 to 3.5
- lengths: int32 [8], P('ctx'), may hold values from 64 to 512, as said below
- offsets: int32 [8], P('ctx'), may hold values from 0 to 8128, as said below
- decay_rates: float32 [16, 1024], P(None, 'chan'), may hold values from 0 to 1, as said below
- residues: float32 [16, 1024], P(None, 'chan'), may hold values from -1 to 1
- skip_weight: float32 [8192], P('chan'), may hold values from -1 to 1
- out_weight: bfloat16 [8192, 4096], P('chan'), may hold values from -0.09375 to 0.09375
Outputs:
- projected: bfloat16 [4096, 4096], P('chan', 'ctx')
Inputs may be any that keep to these rules, and one draw needn't show every extreme that they name: `lengths`: used slots of each shard, counted from slot 0; some shard uses all 512 slots and some only 64. offsets[i] + lengths[i] <= offsets[i + 1]; the first offset is 0. `decay_rates`: positive rates.
All inputs are finite; a program needn't handle non-finite values.
Results may differ from a plain program's by a relative error of at most 0.018.
Values may be sent and summed in bfloat16 or wider, within the bound.
No kernel may reach another device: no remote copies, remote signals or barrier semaphores. Data moves between devices by JAX's collectives and lax.ppermute only.
A program may use at most 192 MiB of HBM per device.

v0:
```python
import jax
import jax.numpy as jnp
from jax import lax
from jax.sharding import PartitionSpec as P

highest = lax.Precision.HIGHEST


def passed_along(array, axis, by):
    length = lax.axis_size(axis)
    pairs = [(i, i + by) for i in range(length) if 0 <= i + by < length]
    return lax.ppermute(array, axis, pairs)


def shortened(array):
    return jax.tree.map(lambda a: a.astype(jnp.bfloat16) if a.dtype == jnp.float32 else a, array)


def block_pass(blocks, firsts, counts, decay_rows, residue):
    groups, per_group, block_count, block_width = blocks.shape
    mode_count = decay_rows.shape[0]
    rate_g = decay_rows.T
    residue_g = residue.T
    lag_index = jnp.arange(block_width)
    lag_float = lag_index.astype(jnp.float32)
    to_end = jnp.exp(-rate_g[:, None, :] * (block_width - 1.0 - lag_float)[None, :, None])
    raw_sums = lax.dot_general(
        blocks.reshape(groups, per_group * block_count, block_width),
        to_end,
        (((2,), (1,)), ((0,), (0,))),
        precision=highest,
    )
    lift = jnp.exp(rate_g[:, None, :] * (block_width - counts.astype(jnp.float32))[None, :, None])
    summary = raw_sums.reshape(groups, per_group, block_count, mode_count) * lift[:, None, :, :]
    difference = (lag_index[:, None] - lag_index[None, :]).astype(jnp.float32)
    distance = jnp.maximum(difference, 0.0)
    toeplitz = jnp.zeros((groups, block_width, block_width), jnp.float32)
    for mode_index in range(mode_count):
        toeplitz = toeplitz + residue_g[:, mode_index, None, None] * jnp.exp(
            -rate_g[:, mode_index, None, None] * distance[None]
        )
    toeplitz = jnp.where((difference >= 0.0)[None], toeplitz, 0.0)
    inner_part = lax.dot_general(blocks, toeplitz, (((3,), (2,)), ((0,), (0,))), precision=highest)
    lasts = firsts + counts.astype(jnp.float32) - 1.0
    gap_matrix = jnp.maximum(firsts[None, :] - lasts[:, None], 0.0)
    earlier_mask = lag_index[:block_count, None] < lag_index[None, :block_count]
    mixing = jnp.where(
        earlier_mask[None, None], jnp.exp(-rate_g[:, :, None, None] * gap_matrix[None, None]), 0.0
    )
    entering = jnp.einsum("gkcm,gmcb->gkbm", summary, mixing, precision=highest)
    return (inner_part, summary, entering, lasts)


def outer_pass(entering, decay_rows, residue, block_width):
    groups, per_group, block_count, mode_count = entering.shape
    rate_g = decay_rows.T
    lag_float = jnp.arange(block_width, dtype=jnp.float32)
    spread_values = residue.T[:, :, None] * jnp.exp(-rate_g[:, :, None] * lag_float[None, None, :])
    outer_part = lax.dot_general(
        entering.reshape(groups, per_group * block_count, mode_count),
        spread_values,
        (((2,), (1,)), ((0,), (0,))),
        precision=highest,
    )
    return outer_part.reshape(groups, per_group, block_count, block_width)


def shards(
    features, short_filter, lengths, offsets, decay_rates, residues, skip_weight, out_weight
):
    kernel_taps = short_filter.shape[1]
    channels = features.shape[1]
    slot_count = features.shape[2]
    groups = decay_rates.shape[1]
    per_group = channels // groups
    block_width = min(128, slot_count)
    length = lengths[0]
    tail_rows = lax.dynamic_slice_in_dim(
        features, length - (kernel_taps - 1), kernel_taps - 1, axis=2
    )
    previous = passed_along(tail_rows, "ctx", 1)
    extended = jnp.concatenate([previous, features], axis=2)
    short_conv = jnp.zeros((3, channels, slot_count), jnp.float32)
    for tap_index in range(kernel_taps):
        window_rows = lax.slice_in_dim(
            extended, kernel_taps - 1 - tap_index, kernel_taps - 1 - tap_index + slot_count, axis=2
        )
        short_conv = short_conv + short_filter[:, tap_index, :, None] * window_rows.astype(
            jnp.float32
        )
    usable = jnp.arange(slot_count) < length
    product = jnp.where(usable, short_conv[1] * short_conv[2], 0.0)
    all_lengths, all_offsets = (
        lax.all_gather(lengths, "ctx", axis=0, tiled=True),
        lax.all_gather(offsets, "ctx", axis=0, tiled=True),
    )
    ctx_count = lax.axis_size("ctx")
    rank_self = lax.axis_index("ctx")
    shared = groups // ctx_count
    decay_mine = lax.dynamic_slice_in_dim(decay_rates, rank_self * shared, shared, 1)
    residue_mine = lax.dynamic_slice_in_dim(residues, rank_self * shared, shared, 1)
    per_shard = slot_count // block_width
    within = jnp.tile(jnp.arange(per_shard) * block_width, ctx_count)
    firsts_all = jnp.repeat(all_offsets, per_shard).astype(jnp.float32) + within.astype(jnp.float32)
    counts_all = jnp.clip(jnp.repeat(all_lengths, per_shard) - within, 0, block_width)
    received = lax.all_to_all(
        product.reshape(groups, per_group, slot_count).astype(jnp.bfloat16),
        "ctx",
        split_axis=0,
        concat_axis=2,
        tiled=True,
    ).astype(jnp.float32)
    item_count = received.shape[1]
    blocks = received.reshape(shared, item_count, ctx_count * per_shard, block_width)
    inner_part, summary, entering, lasts = block_pass(
        blocks, firsts_all, counts_all, decay_mine, residue_mine
    )
    outer_part = outer_pass(entering, decay_mine, residue_mine, block_width)
    result = (inner_part + outer_part).reshape(shared, item_count, ctx_count * slot_count)
    long_conv = lax.all_to_all(
        shortened(result), "ctx", split_axis=2, concat_axis=0, tiled=True
    ).astype(result.dtype)
    long_conv = long_conv.reshape(channels, slot_count)
    mixed_rows = jnp.where(
        usable, short_conv[0] * (long_conv + skip_weight[:, None] * product), 0.0
    ).astype(jnp.bfloat16)
    return lax.psum_scatter(
        lax.dot_general(
            out_weight, mixed_rows, (((0,), (0,)), ((), ())), preferred_element_type=jnp.float32
        ).astype(jnp.bfloat16),
        "chan",
        scatter_dimension=0,
        tiled=True,
    )


def solution(mesh):
    placed = (
        P(None, "chan", "ctx"),
        P(None, None, "chan"),
        P("ctx"),
        P("ctx"),
        P(None, "chan"),
        P(None, "chan"),
        P("chan"),
        P("chan", None),
    )
    return jax.shard_map(
        shards, mesh=mesh, in_specs=placed, out_specs=P("chan", "ctx"), check_vma=False
    )
```

profile of v0, /device:TPU:0, one launch (start us, length us, event | category | flops | bytes accessed | tf_op | source)
XLA Modules:
  0.0 309.9 jit_solution(4460304330251844339)
XLA Ops:
  7.2 2.5 constant_dynamic-slice_fusion
  9.7 0.9 copy.54
  10.6 2.4 collective-permute-start
  13.6 0.6 dynamic-slice
  14.3 0.7 dynamic-update-slice.1
  15.0 0.7 dynamic-update-slice
  15.8 9.1 %all-reduce.2 = (s32[8]{0:T(128)S(1)}, s32[8]{0:T(128)S(1)}) all-reduce(s32[8]{0:T(128)S(1)} %dynamic-update-slice, s32[8]{0:T(128)S(1)} %dynamic-update-slice.1), channel_id=1, replica_groups=mesh['ctx'=8,'chan'=4] {'ctx'}, use_global_device_ids=true, to_apply=%add | all-reduce | flops 16 | bytes 128
  25.1 0.9 copy.38
  26.0 12.5 %multiply_add_fusion = f32[3,2048,512]{2,1,0:T(8,128)S(1)} fusion(bf16[3,2048,512]{2,1,0:T(8,128)(2,1)} %param.8, bf16[3,2048,2]{2,1,0:T(8,128)(2,1)S(1)} %copy.38, f32[3,2048]{1,0:T(4,128)S(1)} %get-tuple-element.46, f32[3,2048]{1,0:T(4,128)S(1)} %get-tuple-element.47, f32[3,2048]{1,0:T(4,128)S(1)} %bitcast.143), kind=kLoop, calls=%fused_computation.1 | loop fusion | flops 44040192 | bytes 18972672 | tf_op jit(solution)/shard_map/add | solution.py:88
  38.5 4.5 %copy-done.2 = f32[3,2048,512]{2,1,0:T(8,128)} copy-done((f32[3,2048,512]{2,1,0:T(8,128)}, f32[3,2048,512]{2,1,0:T(8,128)S(1)}, u32[]{:S(2)}) %copy-start.2) | copy-done | bytes 12582936
  43.1 2.5 fusion.11
  45.5 3.7 %all-to-all-start = ((bf16[256,8,512]{2,1,0:T(8,128)(2,1)}), bf16[256,8,512]{2,1,0:T(8,128)(2,1)S(1)}, u32[]{:S(2)}, u32[]{:S(2)}) async-start(bf16[256,8,512]{2,1,0:T(8,128)(2,1)} %fusion.11), calls=%async_computation | async-start | bytes 4194304 | tf_op jit(solution)/shard_map/all_to_all | solution.py:106
  50.3 25.6 %all-to-all-done = bf16[256,8,512]{2,1,0:T(8,128)(2,1)S(1)} async-done(((bf16[256,8,512]{2,1,0:T(8,128)(2,1)}), bf16[256,8,512]{2,1,0:T(8,128)(2,1)S(1)}, u32[]{:S(2)}, u32[]{:S(2)}) %all-to-all-start) | async-done | bytes 2097184 | tf_op jit(solution)/shard_map/all_to_all | solution.py:106
  75.9 1.3 copy-done.3
  77.2 3.3 %copy.39 = bf16[32,8,8,512]{3,2,1,0:T(8,128)(2,1)S(1)} copy(bf16[32,8,8,512]{3,1,0,2:T(8,128)(2,1)} %bitcast.141) | data formatting | bytes 4194304 | tf_op jit(solution)/shard_map/all_to_all | solution.py:106
  80.5 2.8 reshape_reshape.3
  83.3 2.6 reshape.334
  85.9 3.4 %fusion.128 = f32[32,256,16]{1,2,0:T(8,128)S(1)} fusion(bf16[32,256,128]{2,1,0:T(8,128)(2,1)} %reshape_reshape.3, f32[128]{0:T(128)S(1)} %convert_subtract_fusion, f32[32,16]{1,0:T(8,128)S(1)} %copy.40), kind=kOutput, calls=%fused_computation.136 | convolution fusion | flops 201392128 | bytes 2624000 | tf_op jit(solution)/shard_map/dot_general | solution.py:27
  89.7 17.6 %fusion.82 = f32[32,8,32,16]{2,1,3,0:T(8,128)} fusion(f32[32,8,32,16]{2,1,3,0:T(8,128)S(1)} %reshape.335, f32[32,32]{1,0:T(8,128)S(1)} %subtract_maximum_fusion, f32[32,16]{1,0:T(8,128)S(1)} %copy.40, pred[32,32]{1,0:T(8,128)(4,1)S(1)} %broadcast_compare_fusion, f32[32,32,16]{1,2,0:T(8,128)S(1)} %multiply_exponential_fusion), kind=kOutput, calls=%fused_computation.93 | convolution fusion | flops 51511296 | bytes 1121280 | tf_op jit(solution)/shard_map/gkcm,gmcb->gkbm/dot_general | solution.py:50
  107.3 2.1 reshape.336
  109.5 7.5 %fusion.123 = f32[32,256,128]{2,1,0:T(8,128)S(1)} fusion(f32[32,256,16]{1,2,0:T(8,128)S(1)} %reshape.336, f32[32,16]{1,0:T(8,128)S(1)} %copy.40, f32[32,16]{1,0:T(8,128)S(1)} %copy.44), kind=kOutput, calls=%fused_computation.130 | convolution fusion | flops 201457664 | bytes 4722688 | tf_op jit(solution)/shard_map/dot_general | solution.py:59
  117.0 9.5 %add_convert_fusion = bf16[32,8,32,128]{3,2,1,0:T(8,128)(2,1)S(1)} fusion(f32[32,8,32,128]{3,2,1,0:T(8,128)S(1)} %bitcast.142, bf16[32,8,32,128]{3,2,1,0:T(8,128)(2,1)S(1)} %copy-done.4, f32[32]{0:T(128)S(1)} %get-tuple-element.29, f32[32]{0:T(128)S(1)} %get-tuple-element.13, f32[32]{0:T(128)S(1)} %get-tuple-element.30, f32[32]{0:T(128)S(1)} %get-tuple-element.14, ...), kind=kOutput, calls=%fused_computation.22 | convolution fusion | flops 1637875712 | bytes 8474624 | tf_op jit(solution)/shard_map/dot_general | solution.py:43
  126.5 6.8 %copy.50 = bf16[32,8,32,128]{0,1,3,2:T(8,128)(2,1)} copy(bf16[32,8,32,128]{3,2,1,0:T(8,128)(2,1)S(1)} %add_convert_fusion) | data formatting | bytes 4194304 | tf_op jit(solution)/shard_map/convert_element_type | solution.py:16
  133.3 10.1 %reshape.351 = bf16[8,2,65536]{2,1,0:T(2,128)(2,1)S(1)} reshape(bf16[4096,8,32]{2,1,0:T(8,128)(2,1)} %bitcast.140) | data formatting | bytes 4194304
  143.5 29.8 %all_to_all.24 = bf16[8,2,65536]{2,1,0:T(2,128)(2,1)} all-to-all(bf16[8,2,65536]{2,1,0:T(2,128)(2,1)S(1)} %reshape.351), channel_id=1, replica_groups=mesh['ctx'=8,'chan'=4] {'ctx'}, dimensions={0} | all-to-all | bytes 4194304 | tf_op jit(solution)/shard_map/all_to_all | solution.py:120
  173.2 8.7 %reshape.352 = bf16[4096,8,32]{2,1,0:T(8,128)(2,1)} reshape(bf16[8,2,65536]{2,1,0:T(2,128)(2,1)} %all_to_all.24) | data formatting | bytes 4194304
  181.9 10.2 %convert_bitcast_fusion = f32[8,32,8,512]{1,2,3,0:T(8,128)} fusion(bf16[32,8,8,512]{0,1,3,2:T(8,128)(2,1)} %bitcast.139), kind=kLoop, calls=%fused_computation | loop fusion | flops 1048576 | bytes 6291456 | tf_op jit(solution)/shard_map/convert_element_type | solution.py:122
  192.1 12.0 %copy.47 = f32[8,32,8,512]{3,2,1,0:T(8,128)} copy(f32[8,32,8,512]{1,2,3,0:T(8,128)} %convert_bitcast_fusion) | data formatting | bytes 8388608 | tf_op jit(solution)/shard_map/convert_element_type | solution.py:122
  204.1 6.4 %fusion.8 = bf16[2048,512]{1,0:T(8,128)(2,1)S(1)} fusion(f32[3,2048,512]{2,1,0:T(8,128)} %copy-done.2, f32[8,32,8,512]{3,2,1,0:T(8,128)} %copy.47, f32[2048]{0:T(1024)S(1)} %copy-done.6, pred[512]{0:T(512)(128)(4,1)S(1)} %iota_compare_fusion), kind=kLoop, calls=%fused_computation.16 | loop fusion | flops 7340032 | bytes 18883072 | tf_op jit(solution)/shard_map/convert_element_type | solution.py:126
  210.5 14.0 %fusion.5 = bf16[4096,512]{0,1:T(8,128)(2,1)} fusion(bf16[2048,512]{1,0:T(8,128)(2,1)S(1)} %fusion.8, bf16[2048,4096]{1,0:T(8,128)(2,1)} %param.15), kind=kOutput, calls=%fused_computation.11 | convolution fusion | flops 8592031744 | bytes 23068672 | tf_op jit(solution)/shard_map/dot_general | solution.py:128
  224.5 76.3 %reduce-scatter.2.cloned.1.call-done = bf16[1024,512]{0,1:T(8,128)(2,1)} async-done(((bf16[4096,512]{0,1:T(8,128)(2,1)}), bf16[1024,512]{0,1:T(8,128)(2,1)}) %reduce-scatter.2.cloned.1.call-update) | async-done | bytes 1048592 | tf_op jit(solution)/shard_map/reduce_scatter | solution.py:127
  300.8 2.3 copy.48
  (48 shorter events, 1.7 us)
Async XLA Ops:
  6.5 42.8 %copy-start = (f32[16,256]{1,0:T(8,128)S(1)}, f32[16,256]{1,0:T(8,128)}, u32[]{:S(2)}) copy-start(f32[16,256]{1,0:T(8,128)} %param.13) | copy-start | bytes 49156
  7.2 6.4 %copy-start.8 = (u32[32]{0:T(128)S(1)}, u32[32]{0:T(128)}, u32[]{:S(2)}) copy-start(u32[32]{0:T(128)} %constant.36) | copy-start | bytes 388
  7.2 17.6 %copy-start.5 = (f32[3,3,2048]{2,1,0:T(4,128)S(1)}, f32[3,3,2048]{2,1,0:T(4,128)}, u32[]{:S(2)}) copy-start(f32[3,3,2048]{2,1,0:T(4,128)} %param.9) | copy-start | bytes 221188
  10.6 14.5 %collective-permute-start = (bf16[3,2048,2]{1,0,2:T(4,128)(2,1)S(1)}, bf16[3,2048,2]{1,0,2:T(4,128)(2,1)S(1)}, u32[]{:S(2)}, u32[]{:S(2)}) collective-permute-start(bf16[3,2048,2]{1,0,2:T(4,128)(2,1)S(1)} %copy.54), channel_id=1, source_target_pairs={{0,4},{4,8},{8,12},{12,16},{16,20},{20,24},{24,28},{1,5},{5,9},{9,... | collective-permute-start | bytes 73736 | tf_op jit(solution)/shard_map/ppermute | solution.py:12
  38.5 4.5 %copy-start.2 = (f32[3,2048,512]{2,1,0:T(8,128)}, f32[3,2048,512]{2,1,0:T(8,128)S(1)}, u32[]{:S(2)}) copy-start(f32[3,2048,512]{2,1,0:T(8,128)S(1)} %multiply_add_fusion) | copy-start | bytes 37748740
  45.5 4.1 %copy-start.7 = (f32[16,256]{1,0:T(8,128)S(1)}, f32[16,256]{1,0:T(8,128)}, u32[]{:S(2)}) copy-start(f32[16,256]{1,0:T(8,128)} %param.12) | copy-start | bytes 49156
  45.5 30.3 %all-to-all-start = ((bf16[256,8,512]{2,1,0:T(8,128)(2,1)}), bf16[256,8,512]{2,1,0:T(8,128)(2,1)S(1)}, u32[]{:S(2)}, u32[]{:S(2)}) async-start(bf16[256,8,512]{2,1,0:T(8,128)(2,1)} %fusion.11), calls=%async_computation | async-start | bytes 4194304 | tf_op jit(solution)/shard_map/all_to_all | solution.py:106
  49.3 251.5 %reduce-scatter.2.cloned.1.call-start = ((), (), s32[]{:S(2)}) async-start(), calls=%async_computation.3 | async-start | bytes 5242880 | tf_op jit(solution)/shard_map/reduce_scatter | solution.py:127
  75.9 1.3 copy-start.3
  109.5 7.5 %copy-start.4 = (bf16[32,8,32,128]{3,2,1,0:T(8,128)(2,1)S(1)}, bf16[32,8,32,128]{3,2,1,0:T(8,128)(2,1)}, u32[]{:S(2)}) copy-start(bf16[32,8,32,128]{3,2,1,0:T(8,128)(2,1)} %reshape.334) | copy-start | bytes 6291460
  192.1 12.0 %copy-start.6 = (f32[2048]{0:T(1024)S(1)}, f32[2048]{0:T(1024)}, u32[]{:S(2)}) copy-start(f32[2048]{0:T(1024)} %param.14) | copy-start | bytes 24580
  224.5 78.6 %copy-start.1 = (f32[16,256]{1,0:T(8,128)S(1)}, f32[16,256]{1,0:T(8,128)}, u32[]{:S(2)}) copy-start(f32[16,256]{1,0:T(8,128)} %param.13) | copy-start | bytes 49156
Sparse Core Ops, SparseCore 0:
  224.6 76.1 reduce-scatter.1
where the time goes:
time: 311 us; the launch traced here: 310 us
  waiting for transfers between devices  102 us (33%)
  local copies, waits for them, and re-layouts  63.9 us (21%)
  matrix products  52 us (17%)
  blocking collectives  38.8 us (12%)
  other arithmetic  32.2 us (10%)
  between operations  15 us (5%)
  starting transfers between devices  6.13 us (2%)
    reduce_scatter x1, waiting for transfers between devices, shards(): lax.psum_scatter(lax.dot_general(out_weight, mixed_rows, (((0,), (0,)), (...  76.3 us
    all_to_all x1, blocking collectives, shards(): lax.all_to_all(shortened(result), 'ctx', split_axis=2, concat_axis=0, til...  29.8 us
    unnamed x28, local copies, waits for them, and re-layouts  27.7 us
    all_to_all x1, waiting for transfers between devices, shards(): lax.all_to_all(product.reshape(groups, per_group, slot_count).astype(jnp....  25.6 us
    dot_general x1, matrix products, block_pass(): entering = jnp.einsum('gkcm,gmcb->gkbm', summary, mixing, precision=highest)  17.6 us
    dot_general x1, matrix products, shards(): lax.dot_general(out_weight, mixed_rows, (((0,), (0,)), ((), ())), preferr...  14 us
    add x1, other arithmetic, shards(): short_conv + short_filter[:, tap_index, :, None] * window_rows.astype(jnp...  12.5 us
    convert_element_type x1, local copies, waits for them, and re-layouts, shards(): long_conv = lax.all_to_all(shortened(result), 'ctx', split_axis=2, concat...  12 us
  transfers between devices with their start and end apart: 3, of which 2 were waited for; matrix products, arithmetic and copies ran while one was open for 1% of the time, Pallas kernels for 0%

commit v1 on v0

--- a/solution.py
+++ b/solution.py
@@ -117,8 +117,11 @@
     )
     outer_part = outer_pass(entering, decay_mine, residue_mine, block_width)
     result = (inner_part + outer_part).reshape(shared, item_count, ctx_count * slot_count)
-    long_conv = lax.all_to_all(
-        shortened(result), "ctx", split_axis=2, concat_axis=0, tiled=True
+    long_conv = jnp.concatenate(
+        lax.all_to_all(
+            jnp.stack(jnp.split(shortened(result), lax.axis_size("ctx"), axis=2)), "ctx", 0, 0
+        ),
+        axis=0,
     ).astype(result.dtype)
     long_conv = long_conv.reshape(channels, slot_count)
     mixed_rows = jnp.where(

time: 311 us -> 265 us (0.85)
  local copies, waits for them, and re-layouts: 63.9 us -> 29.3 us
  other arithmetic: 32.2 us -> 15.7 us
  matrix products: 52 us -> 58.4 us
    unnamed x28 -> x33, local copies, waits for them, and re-layouts: 27.7 us -> 9.05 us
    convert_element_type x2 -> x0, other arithmetic: 16.6 us -> none  [the longest x1 10.2 us: shards(): long_conv = lax.all_to_all(shortened(result), 'ctx', split_axis=2, concat...]
    convert_element_type x1 -> x0, local copies, waits for them, and re-layouts: 12 us -> none  [shards(): long_conv = lax.all_to_all(shortened(result), 'ctx', split_axis=2, concat...]
    dot_general x1, matrix products: 14 us -> 20.2 us  [shards(): lax.dot_general(out_weight, mixed_rows, (((0,), (0,)), ((), ())), preferr...]
    convert_element_type x1, local copies, waits for them, and re-layouts: 6.8 us -> 2.82 us  [shortened(): a.astype(jnp.bfloat16)]
where the time goes in v1:
time: 265 us
  waiting for transfers between devices  102 us (38%)
  matrix products  58.4 us (22%)
  blocking collectives  38.1 us (14%)
  local copies, waits for them, and re-layouts  29.3 us (11%)
  other arithmetic  15.7 us (6%)
  between operations  15 us (6%)
  starting transfers between devices  6.13 us (2%)
    reduce_scatter x1, waiting for transfers between devices, shards(): lax.psum_scatter(lax.dot_general(out_weight, mixed_rows, (((0,), (0,)), (...  76.3 us
    all_to_all x1, blocking collectives, shards(): lax.all_to_all(jnp.stack(jnp.split(shortened(result), lax.axis_size('ctx'...  29 us
    all_to_all x1, waiting for transfers between devices, shards(): lax.all_to_all(product.reshape(groups, per_group, slot_count).astype(jnp....  25.6 us
    dot_general x1, matrix products, shards(): lax.dot_general(out_weight, mixed_rows, (((0,), (0,)), ((), ())), preferr...  20.2 us
    dot_general x1, matrix products, block_pass(): entering = jnp.einsum('gkcm,gmcb->gkbm', summary, mixing, precision=highest)  17.7 us
    add x1, other arithmetic, shards(): short_conv + short_filter[:, tap_index, :, None] * window_rows.astype(jnp...  12.6 us
    dot_general x1, matrix products, block_pass(): lax.dot_general(blocks, toeplitz, (((3,), (2,)), ((0,), (0,))), precision...  9.64 us
    unnamed x33, local copies, waits for them, and re-layouts  9.05 us
  transfers between devices with their start and end apart: 3, of which 2 were waited for; matrix products, arithmetic and copies ran while one was open for 1% of the time, Pallas kernels for 0%

profile of v1, /device:TPU:0, one launch (start us, length us, event | category | flops | bytes accessed | tf_op | source)
XLA Modules:
  0.0 264.5 jit_solution(9680521514836836407)
XLA Ops:
  7.2 2.5 constant_dynamic-slice_fusion
  9.7 0.9 copy.37
  10.6 2.4 collective-permute-start
  13.6 0.6 dynamic-slice
  14.3 0.7 dynamic-update-slice.1
  15.0 0.7 dynamic-update-slice
  15.8 9.1 %all-reduce.2 = (s32[8]{0:T(128)S(1)}, s32[8]{0:T(128)S(1)}) all-reduce(s32[8]{0:T(128)S(1)} %dynamic-update-slice, s32[8]{0:T(128)S(1)} %dynamic-update-slice.1), channel_id=1, replica_groups=mesh['ctx'=8,'chan'=4] {'ctx'}, use_global_device_ids=true, to_apply=%add | all-reduce | flops 16 | bytes 128
  25.1 0.9 copy.24
  26.0 12.6 %multiply_add_fusion = f32[3,2048,512]{2,1,0:T(8,128)S(1)} fusion(bf16[3,2048,512]{2,1,0:T(8,128)(2,1)} %param.8, bf16[3,2048,2]{2,1,0:T(8,128)(2,1)S(1)} %copy.24, f32[3,2048]{1,0:T(4,128)S(1)} %get-tuple-element.46, f32[3,2048]{1,0:T(4,128)S(1)} %get-tuple-element.47, f32[3,2048]{1,0:T(4,128)S(1)} %bitcast.168), kind=kLoop, calls=%fused_computation | loop fusion | flops 44040192 | bytes 18972672 | tf_op jit(solution)/shard_map/add | solution.py:88
  38.6 4.5 %copy-done.2 = f32[3,2048,512]{2,1,0:T(8,128)} copy-done((f32[3,2048,512]{2,1,0:T(8,128)}, f32[3,2048,512]{2,1,0:T(8,128)S(1)}, u32[]{:S(2)}) %copy-start.2) | copy-done | bytes 12582936
  43.1 2.5 fusion.10
  45.6 3.7 %all-to-all-start = ((bf16[256,8,512]{2,1,0:T(8,128)(2,1)}), bf16[256,8,512]{2,1,0:T(8,128)(2,1)S(1)}, u32[]{:S(2)}, u32[]{:S(2)}) async-start(bf16[256,8,512]{2,1,0:T(8,128)(2,1)} %fusion.10), calls=%async_computation | async-start | bytes 4194304 | tf_op jit(solution)/shard_map/all_to_all | solution.py:106
  49.4 0.1 dynamic-slice_bitcast_fusion.1
  49.5 0.1 convert_element_type.133
  49.6 0.1 add.115
  50.3 0.1 multiply_exponential_fusion
  50.4 25.6 %all-to-all-done = bf16[256,8,512]{2,1,0:T(8,128)(2,1)S(1)} async-done(((bf16[256,8,512]{2,1,0:T(8,128)(2,1)}), bf16[256,8,512]{2,1,0:T(8,128)(2,1)S(1)}, u32[]{:S(2)}, u32[]{:S(2)}) %all-to-all-start) | async-done | bytes 2097184 | tf_op jit(solution)/shard_map/all_to_all | solution.py:106
  76.0 1.3 copy-done.3
  77.3 3.3 %copy.25 = bf16[32,8,8,512]{3,2,1,0:T(8,128)(2,1)S(1)} copy(bf16[32,8,8,512]{3,1,0,2:T(8,128)(2,1)} %bitcast.165) | data formatting | bytes 4194304 | tf_op jit(solution)/shard_map/all_to_all | solution.py:106
  80.6 2.8 %reshape_reshape.3 = bf16[32,256,128]{2,1,0:T(8,128)(2,1)} reshape(bf16[32,8,8,512]{3,2,1,0:T(8,128)(2,1)S(1)} %copy.25) | data formatting | bytes 4194304 | tf_op jit(solution)/shard_map/reshape;reshape | solution.py:28
  83.4 2.6 reshape.333
  86.0 3.4 %fusion.139 = f32[32,256,16]{1,2,0:T(8,128)S(1)} fusion(bf16[32,256,128]{2,1,0:T(8,128)(2,1)} %reshape_reshape.3, f32[128]{0:T(128)S(1)} %convert_subtract_fusion, f32[32,16]{1,0:T(8,128)S(1)} %copy.26), kind=kOutput, calls=%fused_computation.154 | convolution fusion | flops 201392128 | bytes 2624000 | tf_op jit(solution)/shard_map/dot_general | solution.py:27
  89.4 0.5 reshape.334
  89.9 17.7 %fusion.85 = f32[32,8,32,16]{2,1,3,0:T(8,128)} fusion(f32[32,8,32,16]{2,1,3,0:T(8,128)S(1)} %reshape.334, f32[32,32]{1,0:T(8,128)S(1)} %subtract_maximum_fusion, f32[32,16]{1,0:T(8,128)S(1)} %copy.26, pred[32,32]{1,0:T(8,128)(4,1)S(1)} %broadcast_compare_fusion, f32[32,32,16]{1,2,0:T(8,128)S(1)} %multiply_exponential_fusion), kind=kOutput, calls=%fused_computation.95 | convolution fusion | flops 51511296 | bytes 1121280 | tf_op jit(solution)/shard_map/gkcm,gmcb->gkbm/dot_general | solution.py:50
  107.5 2.1 reshape.335
  109.7 7.5 %fusion.134 = f32[32,256,128]{2,1,0:T(8,128)S(1)} fusion(f32[32,256,16]{1,2,0:T(8,128)S(1)} %reshape.335, f32[32,16]{1,0:T(8,128)S(1)} %copy.26, f32[32,16]{1,0:T(8,128)S(1)} %copy.30), kind=kOutput, calls=%fused_computation.148 | convolution fusion | flops 201457664 | bytes 4722688 | tf_op jit(solution)/shard_map/dot_general | solution.py:59
  117.2 9.6 %add_convert_fusion = bf16[32,8,32,128]{3,2,1,0:T(8,128)(2,1)} fusion(f32[32,8,32,128]{3,2,1,0:T(8,128)S(1)} %bitcast.166, bf16[32,8,32,128]{3,2,1,0:T(8,128)(2,1)S(1)} %copy-done.4, f32[32]{0:T(128)S(1)} %get-tuple-element.29, f32[32]{0:T(128)S(1)} %get-tuple-element.13, f32[32]{0:T(128)S(1)} %get-tuple-element.30, f32[32]{0:T(128)S(1)} %get-tuple-element.14, ...), kind=kOutput, calls=%fused_computation.21 | convolution fusion | flops 1637875712 | bytes 8474624 | tf_op jit(solution)/shard_map/dot_general | solution.py:43
  126.8 2.8 %convert_element_type.136 = bf16[32,8,4096]{2,1,0:T(8,128)(2,1)S(1)} reshape(bf16[32,8,32,128]{3,2,1,0:T(8,128)(2,1)} %add_convert_fusion) | data formatting | bytes 4194304 | tf_op jit(solution)/shard_map/convert_element_type | solution.py:16
  129.9 29.0 %all_to_all.20 = bf16[8,32,8,512]{3,2,1,0:T(8,128)(2,1)S(1)} all-to-all(bf16[8,32,8,512]{3,2,1,0:T(8,128)(2,1)S(1)} %fusion.126), channel_id=1, replica_groups=mesh['ctx'=8,'chan'=4] {'ctx'}, dimensions={0} | all-to-all | bytes 4194304 | tf_op jit(solution)/shard_map/all_to_all | solution.py:121
  158.9 20.2 %fusion.5 = bf16[4096,512]{0,1:T(8,128)(2,1)} fusion(bf16[2048,4096]{1,0:T(8,128)(2,1)} %param.15, f32[3,2048,512]{2,1,0:T(8,128)} %copy-done.2, bf16[2048,512]{1,0:T(8,128)(2,1)S(1)} %bitcast.167, f32[2048]{0:T(1024)S(1)} %copy-done.7, pred[512]{0:T(512)(128)(4,1)S(1)} %iota_compare_fusion), kind=kOutput, calls=%fused_computation.10 | convolution fusion | flops 8600420352 | bytes 35660288 | tf_op jit(solution)/shard_map/dot_general | solution.py:131
  179.2 76.3 %reduce-scatter.2.cloned.1.call-done = bf16[1024,512]{0,1:T(8,128)(2,1)} async-done(((bf16[4096,512]{0,1:T(8,128)(2,1)}), bf16[1024,512]{0,1:T(8,128)(2,1)}) %reduce-scatter.2.cloned.1.call-update) | async-done | bytes 1048592 | tf_op jit(solution)/shard_map/reduce_scatter | solution.py:130
  255.4 2.3 copy.32
  (51 shorter events, 1.0 us)
Async XLA Ops:
  6.5 42.9 %copy-start = (f32[16,256]{1,0:T(8,128)S(1)}, f32[16,256]{1,0:T(8,128)}, u32[]{:S(2)}) copy-start(f32[16,256]{1,0:T(8,128)} %param.13) | copy-start | bytes 49156
  7.2 6.4 %copy-start.8 = (u32[32]{0:T(128)S(1)}, u32[32]{0:T(128)}, u32[]{:S(2)}) copy-start(u32[32]{0:T(128)} %constant.36) | copy-start | bytes 388
  7.2 17.6 %copy-start.5 = (f32[3,3,2048]{2,1,0:T(4,128)S(1)}, f32[3,3,2048]{2,1,0:T(4,128)}, u32[]{:S(2)}) copy-start(f32[3,3,2048]{2,1,0:T(4,128)} %param.9) | copy-start | bytes 221188
  10.6 14.5 %collective-permute-start = (bf16[3,2048,2]{1,0,2:T(4,128)(2,1)S(1)}, bf16[3,2048,2]{1,0,2:T(4,128)(2,1)S(1)}, u32[]{:S(2)}, u32[]{:S(2)}) collective-permute-start(bf16[3,2048,2]{1,0,2:T(4,128)(2,1)S(1)} %copy.37), channel_id=1, source_target_pairs={{0,4},{4,8},{8,12},{12,16},{16,20},{20,24},{24,28},{1,5},{5,9},{9,... | collective-permute-start | bytes 73736 | tf_op jit(solution)/shard_map/ppermute | solution.py:12
  38.6 4.5 %copy-start.2 = (f32[3,2048,512]{2,1,0:T(8,128)}, f32[3,2048,512]{2,1,0:T(8,128)S(1)}, u32[]{:S(2)}) copy-start(f32[3,2048,512]{2,1,0:T(8,128)S(1)} %multiply_add_fusion) | copy-start | bytes 37748740
  45.6 4.1 %copy-start.6 = (f32[16,256]{1,0:T(8,128)S(1)}, f32[16,256]{1,0:T(8,128)}, u32[]{:S(2)}) copy-start(f32[16,256]{1,0:T(8,128)} %param.12) | copy-start | bytes 49156
  45.6 30.3 %all-to-all-start = ((bf16[256,8,512]{2,1,0:T(8,128)(2,1)}), bf16[256,8,512]{2,1,0:T(8,128)(2,1)S(1)}, u32[]{:S(2)}, u32[]{:S(2)}) async-start(bf16[256,8,512]{2,1,0:T(8,128)(2,1)} %fusion.10), calls=%async_computation | async-start | bytes 4194304 | tf_op jit(solution)/shard_map/all_to_all | solution.py:106
  49.4 206.0 %reduce-scatter.2.cloned.1.call-start = ((), (), s32[]{:S(2)}) async-start(), calls=%async_computation.3 | async-start | bytes 5242880 | tf_op jit(solution)/shard_map/reduce_scatter | solution.py:130
  76.0 1.3 copy-start.3
  109.6 7.5 %copy-start.4 = (bf16[32,8,32,128]{3,2,1,0:T(8,128)(2,1)S(1)}, bf16[32,8,32,128]{3,2,1,0:T(8,128)(2,1)}, u32[]{:S(2)}) copy-start(bf16[32,8,32,128]{3,2,1,0:T(8,128)(2,1)} %reshape.333) | copy-start | bytes 6291460
  129.9 29.1 %copy-start.7 = (f32[2048]{0:T(1024)S(1)}, f32[2048]{0:T(1024)}, u32[]{:S(2)}) copy-start(f32[2048]{0:T(1024)} %param.14) | copy-start | bytes 24580
  179.1 78.6 %copy-start.1 = (f32[16,256]{1,0:T(8,128)S(1)}, f32[16,256]{1,0:T(8,128)}, u32[]{:S(2)}) copy-start(f32[16,256]{1,0:T(8,128)} %param.13) | copy-start | bytes 49156
Sparse Core Ops, SparseCore 0:
  179.3 76.1 reduce-scatter.1
